TPU v7x, 32 devices: a whole 2x2x4 slice. The times are simulated.
32 devices in a mesh: dp: 8 (over y, x, core), tensor: 4 (over z).
Axes of the slice: x: 2, y: 2, z: 4, core: 2. Of those that a mesh axis runs over, the one named last changes fastest.
Arguments:
- tokens: bfloat16 [8, 1024, 1280], P('dp', 'tensor'), may hold values from -6 to 6
- lengths: int32 [8], P('dp'), may hold values from 256 to 1024, as said below
- cotangent: bfloat16 [8, 1024, 1280], P('dp', 'tensor'), may hold values from -6 to 6
- ln1_gain: bfloat16 [1280], P('dp'), may hold values from 0.099609375 to 1.8984375
- ln1_bias: bfloat16 [1280], P('dp'), may hold values from -3 to 3
- query_weight: bfloat16 [1280, 1280], P('dp', 'tensor'), may hold values from -0.25 to 0.25
- query_bias: bfloat16 [1280], P('tensor'), may hold values from -3 to 3
- key_weight: bfloat16 [1280, 1280], P('dp', 'tensor'), may hold values from -0.25 to 0.25
- value_weight: bfloat16 [1280, 1280], P('dp', 'tensor'), may hold values from -0.15625 to 0.15625
- value_bias: bfloat16 [1280], P('tensor'), may hold values from -3 to 3
- out_weight: bfloat16 [1280, 1280], P('dp', 'tensor'), may hold values from -1.25 to 1.25
- out_bias: bfloat16 [1280], P('dp'), may hold values from -3 to 3
- ln2_gain: bfloat16 [1280], P('dp'), may hold values from 0.099609375 to 1.8984375
- ln2_bias: bfloat16 [1280], P('dp'), may hold values from -3 to 3
- up_weight: bfloat16 [1280, 5120], P('dp', 'tensor'), may hold values from -0.15625 to 0.15625
- up_bias: bfloat16 [5120], P('tensor'), may hold values from -3 to 3
- down_weight: bfloat16 [1280, 5120], P('dp', 'tensor'), may hold values from -0.25 to 0.25
- down_bias: bfloat16 [1280], P('dp'), may hold values from -3 to 3
Outputs:
- output: bfloat16 [8, 1024, 1280], P('dp', 'tensor')
- tokens_grad: float32 [8, 1024, 1280], P('dp', 'tensor')
- ln1_gain_grad: float32 [1280], P('dp')
- ln1_bias_grad: float32 [1280], P('dp')
- query_weight_grad: float32 [1280, 1280], P('dp', 'tensor')
- query_bias_grad: float32 [1280], P('tensor')
- key_weight_grad: float32 [1280, 1280], P('dp', 'tensor')
- value_weight_grad: float32 [1280, 1280], P('dp', 'tensor')
- value_bias_grad: float32 [1280], P('tensor')
- out_weight_grad: float32 [1280, 1280], P('dp', 'tensor')
- out_bias_grad: float32 [1280], P('dp')
- ln2_gain_grad: float32 [1280], P('dp')
- ln2_bias_grad: float32 [1280], P('dp')
- up_weight_grad: float32 [1280, 5120], P('dp', 'tensor')
- up_bias_grad: float32 [5120], P('tensor')
- down_weight_grad: float32 [1280, 5120], P('dp', 'tensor')
- down_bias_grad: float32 [1280], P('dp')
Inputs may be any that keep to these rules, and one draw needn't show every extreme that they name: `lengths`: positions of a clip at or past its length are padding and are masked as keys; some clip has exactly 1024 valid positions and some exactly 256.
All inputs are finite; a program needn't handle non-finite values.
Results may differ from a plain program's by a relative error of at most 0.02.
Values may be sent and summed in bfloat16 or wider, within the bound.
No kernel may reach another device: no remote copies, remote signals or barrier semaphores. Data moves between devices by JAX's collectives and lax.ppermute only.
A program may use at most 128 MiB of HBM per device.

v0:
```python
import jax
import jax.numpy as jnp
from jax import lax
from jax.sharding import PartitionSpec as P

HEAD_DIM = 80
masked_score = -1e30


def layer_norm(values, gain, shift):
    centre = values - jnp.mean(values, axis=-1, keepdims=True)
    spread = jnp.mean(centre * centre, axis=-1, keepdims=True)
    return centre * lax.rsqrt(spread + 1e-05) * gain + shift


def masked_scores(query_part, key_rows, length, scale):
    seq = key_rows.shape[0]
    valid = lax.broadcasted_iota(jnp.int32, (seq,), 0) < length
    scores = (
        jnp.einsum("qhe,khe->hqk", query_part, key_rows, preferred_element_type=jnp.float32) * scale
    )
    return jnp.where(valid[None, None, :], scores, masked_score)


def attend_clip(query_rows, key_rows, value_rows, length, blocks):
    seq, heads = (query_rows.shape[0], query_rows.shape[1])
    scale = HEAD_DIM ** (-0.5)
    query_blocks = query_rows.reshape(blocks, seq // blocks, heads, HEAD_DIM)

    def one_block(query_part):
        scores = masked_scores(query_part, key_rows, length, scale)
        top = jnp.max(scores, axis=-1, keepdims=True)
        expo = jnp.exp(scores - top)
        total = jnp.sum(expo, axis=-1, keepdims=True)
        probs = (expo / total).astype(jnp.bfloat16)
        context = jnp.einsum(
            "hqk,khe->qhe", probs, value_rows, preferred_element_type=jnp.float32
        ).astype(jnp.bfloat16)
        return (context, (top + jnp.log(total))[..., 0])

    context, log_total = lax.map(one_block, query_blocks)
    return (context.reshape(seq, heads, HEAD_DIM), log_total)


def attend_back(query_rows, key_rows, value_rows, context_grad, log_total, length, blocks):
    seq, heads = (query_rows.shape[0], query_rows.shape[1])
    scale = HEAD_DIM ** (-0.5)
    query_blocks = query_rows.reshape(blocks, seq // blocks, heads, HEAD_DIM)
    grad_blocks = context_grad.reshape(blocks, seq // blocks, heads, HEAD_DIM)

    def one_block(carry, inputs):
        key_acc, value_acc = carry
        query_part, grad_part, lse_part = inputs
        scores = masked_scores(query_part, key_rows, length, scale)
        probs = jnp.exp(scores - lse_part[..., None])
        value_acc = value_acc + jnp.einsum(
            "hqk,qhe->khe",
            probs.astype(jnp.bfloat16),
            grad_part,
            preferred_element_type=jnp.float32,
        )
        prob_grad = jnp.einsum(
            "qhe,khe->hqk", grad_part, value_rows, preferred_element_type=jnp.float32
        )
        centred = prob_grad - jnp.sum(probs * prob_grad, axis=-1, keepdims=True)
        score_grad = (probs * centred).astype(jnp.bfloat16)
        query_grad = (
            jnp.einsum("hqk,khe->qhe", score_grad, key_rows, preferred_element_type=jnp.float32)
            * scale
        )
        key_acc = (
            key_acc
            + jnp.einsum("hqk,qhe->khe", score_grad, query_part, preferred_element_type=jnp.float32)
            * scale
        )
        return ((key_acc, value_acc), query_grad.astype(jnp.bfloat16))

    zeros = jnp.zeros((seq, heads, HEAD_DIM), jnp.float32)
    (key_acc, value_acc), query_grad = lax.scan(
        one_block, (zeros, zeros), (query_blocks, grad_blocks, log_total)
    )
    return (
        query_grad.reshape(seq, heads, HEAD_DIM),
        key_acc.astype(jnp.bfloat16),
        value_acc.astype(jnp.bfloat16),
    )


def forward_pass(tokens, lengths, weights):
    (
        ln1_gain,
        ln1_bias,
        query_weight,
        query_bias,
        key_weight,
        value_weight,
        value_bias,
        out_weight,
        out_bias,
        ln2_gain,
        ln2_bias,
        up_weight,
        up_bias,
        down_weight,
        down_bias,
    ) = weights
    query_full, key_full, value_full, out_full, gain_one, bias_one, out_shift = (
        lax.all_gather(query_weight, "dp", axis=0, tiled=True),
        lax.all_gather(key_weight, "dp", axis=0, tiled=True),
        lax.all_gather(value_weight, "dp", axis=0, tiled=True),
        lax.all_gather(out_weight, "dp", axis=0, tiled=True),
        lax.all_gather(ln1_gain, "dp", axis=0, tiled=True),
        lax.all_gather(ln1_bias, "dp", axis=0, tiled=True),
        lax.all_gather(out_bias, "dp", axis=0, tiled=True),
    )
    gain_one = gain_one.astype(jnp.float32)
    bias_one = bias_one.astype(jnp.float32)
    rows = tokens.astype(jnp.float32)
    normed = layer_norm(rows, gain_one, bias_one).astype(jnp.bfloat16)
    normed_all = lax.all_gather(normed, "tensor", axis=1, tiled=True)
    clips, seq = (normed_all.shape[0], normed_all.shape[1])
    heads = query_full.shape[1] // HEAD_DIM
    blocks = seq // 512
    shaped = (clips, seq, heads, HEAD_DIM)
    queries = (
        (
            jnp.einsum("csd,dh->csh", normed_all, query_full, preferred_element_type=jnp.float32)
            + query_bias.astype(jnp.float32)
        )
        .astype(jnp.bfloat16)
        .reshape(shaped)
    )
    keyed = (
        jnp.einsum("csd,dh->csh", normed_all, key_full, preferred_element_type=jnp.float32)
        .astype(jnp.bfloat16)
        .reshape(shaped)
    )
    valued = (
        (
            jnp.einsum("csd,dh->csh", normed_all, value_full, preferred_element_type=jnp.float32)
            + value_bias.astype(jnp.float32)
        )
        .astype(jnp.bfloat16)
        .reshape(shaped)
    )

    def clip_attend(item):
        return attend_clip(item[0], item[1], item[2], item[3], blocks)

    context, log_total = lax.map(clip_attend, (queries, keyed, valued, lengths))
    context = context.reshape(clips, seq, heads * HEAD_DIM)
    attn_terms = jnp.einsum("csh,dh->csd", context, out_full, preferred_element_type=jnp.float32)
    attended = lax.psum_scatter(
        attn_terms.astype(jnp.bfloat16), "tensor", scatter_dimension=1, tiled=True
    ).astype(jnp.float32)
    middle = rows + attended + out_shift.astype(jnp.float32)
    up_full, down_full, gain_two, bias_two, down_shift = (
        lax.all_gather(up_weight, "dp", axis=0, tiled=True),
        lax.all_gather(down_weight, "dp", axis=0, tiled=True),
        lax.all_gather(ln2_gain, "dp", axis=0, tiled=True),
        lax.all_gather(ln2_bias, "dp", axis=0, tiled=True),
        lax.all_gather(down_bias, "dp", axis=0, tiled=True),
    )
    gain_two = gain_two.astype(jnp.float32)
    bias_two = bias_two.astype(jnp.float32)
    normed_two = layer_norm(middle, gain_two, bias_two).astype(jnp.bfloat16)
    normed_two_all = lax.all_gather(normed_two, "tensor", axis=1, tiled=True)
    hidden_pre = jnp.einsum(
        "csd,df->csf", normed_two_all, up_full, preferred_element_type=jnp.float32
    ) + up_bias.astype(jnp.float32)
    hidden = jax.nn.gelu(hidden_pre, approximate=False).astype(jnp.bfloat16)
    mlp_terms = jnp.einsum("csf,df->csd", hidden, down_full, preferred_element_type=jnp.float32)
    mixed = lax.psum_scatter(
        mlp_terms.astype(jnp.bfloat16), "tensor", scatter_dimension=1, tiled=True
    ).astype(jnp.float32)
    output = middle + mixed + down_shift.astype(jnp.float32)
    return {
        "output": output,
        "rows": rows,
        "normed_all": normed_all,
        "queries": queries,
        "keyed": keyed,
        "valued": valued,
        "context": context,
        "log_total": log_total,
        "middle": middle,
        "normed_two_all": normed_two_all,
        "hidden_pre": hidden_pre,
        "hidden": hidden,
        "query_full": query_full,
        "key_full": key_full,
        "value_full": value_full,
        "out_full": out_full,
        "up_full": up_full,
        "down_full": down_full,
        "gain_one": gain_one,
        "bias_one": bias_one,
        "gain_two": gain_two,
        "bias_two": bias_two,
        "blocks": blocks,
    }


def local(
    tokens,
    lengths,
    cotangent,
    ln1_gain,
    ln1_bias,
    query_weight,
    query_bias,
    key_weight,
    value_weight,
    value_bias,
    out_weight,
    out_bias,
    ln2_gain,
    ln2_bias,
    up_weight,
    up_bias,
    down_weight,
    down_bias,
):
    weights = (
        ln1_gain,
        ln1_bias,
        query_weight,
        query_bias,
        key_weight,
        value_weight,
        value_bias,
        out_weight,
        out_bias,
        ln2_gain,
        ln2_bias,
        up_weight,
        up_bias,
        down_weight,
        down_bias,
    )
    first = forward_pass(tokens, lengths, weights)
    fenced_tokens, fenced_lengths, fenced_weights, fenced_output = lax.optimization_barrier(
        (tokens, lengths, weights, first["output"])
    )
    saved = forward_pass(fenced_tokens, fenced_lengths, fenced_weights)
    blocks = saved["blocks"]
    grad_out = cotangent.astype(jnp.float32)
    down_shift_grad = jnp.sum(grad_out, axis=(0, 1))
    grad_out_all = lax.all_gather(cotangent, "tensor", axis=1, tiled=True)
    down_grad = jnp.einsum(
        "csd,csf->df", grad_out_all, saved["hidden"], preferred_element_type=jnp.float32
    )
    hidden_grad = jnp.einsum(
        "csd,df->csf", grad_out_all, saved["down_full"], preferred_element_type=jnp.float32
    )
    gelu_pull = jax.vjp(lambda pre: jax.nn.gelu(pre, approximate=False), saved["hidden_pre"])[1]
    pre_grad = gelu_pull(hidden_grad)[0].astype(jnp.bfloat16)
    up_shift_grad = jnp.sum(pre_grad, axis=(0, 1), dtype=jnp.float32)
    up_grad = jnp.einsum(
        "csd,csf->df", saved["normed_two_all"], pre_grad, preferred_element_type=jnp.float32
    )
    up_grad_shard, down_grad_shard = (
        lax.psum_scatter(
            up_grad.astype(jnp.bfloat16), "dp", scatter_dimension=0, tiled=True
        ).astype(jnp.float32),
        lax.psum_scatter(
            down_grad.astype(jnp.bfloat16), "dp", scatter_dimension=0, tiled=True
        ).astype(jnp.float32),
    )
    normed_two_terms = jnp.einsum(
        "csf,df->csd", pre_grad, saved["up_full"], preferred_element_type=jnp.float32
    )
    normed_two_grad = lax.psum_scatter(
        normed_two_terms.astype(jnp.bfloat16), "tensor", scatter_dimension=1, tiled=True
    ).astype(jnp.float32)
    norm_pull = jax.vjp(layer_norm, saved["middle"], saved["gain_two"], saved["bias_two"])[1]
    middle_part, gain_two_grad, bias_two_grad = norm_pull(normed_two_grad)
    middle_grad = grad_out + middle_part
    out_shift_grad = jnp.sum(middle_grad, axis=(0, 1))
    middle_all = lax.all_gather(middle_grad.astype(jnp.bfloat16), "tensor", axis=1, tiled=True)
    out_grad = jnp.einsum(
        "csd,csh->dh", middle_all, saved["context"], preferred_element_type=jnp.float32
    )
    context_grad = jnp.einsum(
        "csd,dh->csh", middle_all, saved["out_full"], preferred_element_type=jnp.float32
    ).astype(jnp.bfloat16)
    queries = saved["queries"]
    clips, seq, heads = (queries.shape[0], queries.shape[1], queries.shape[2])

    def clip_back(item):
        return attend_back(item[0], item[1], item[2], item[3], item[4], item[5], blocks)

    query_grad, key_grad, value_grad = lax.map(
        clip_back,
        (
            queries,
            saved["keyed"],
            saved["valued"],
            context_grad.reshape(clips, seq, heads, HEAD_DIM),
            saved["log_total"],
            lengths,
        ),
    )
    flat = (clips, seq, heads * HEAD_DIM)
    query_grad = query_grad.reshape(flat)
    key_grad = key_grad.reshape(flat)
    value_grad = value_grad.reshape(flat)
    normed_all = saved["normed_all"]
    query_weight_grad = jnp.einsum(
        "csd,csh->dh", normed_all, query_grad, preferred_element_type=jnp.float32
    )
    key_weight_grad = jnp.einsum(
        "csd,csh->dh", normed_all, key_grad, preferred_element_type=jnp.float32
    )
    value_weight_grad = jnp.einsum(
        "csd,csh->dh", normed_all, value_grad, preferred_element_type=jnp.float32
    )
    query_shift_grad = jnp.sum(query_grad, axis=(0, 1), dtype=jnp.float32)
    value_shift_grad = jnp.sum(value_grad, axis=(0, 1), dtype=jnp.float32)
    normed_terms = (
        jnp.einsum(
            "csh,dh->csd", query_grad, saved["query_full"], preferred_element_type=jnp.float32
        )
        + jnp.einsum("csh,dh->csd", key_grad, saved["key_full"], preferred_element_type=jnp.float32)
        + jnp.einsum(
            "csh,dh->csd", value_grad, saved["value_full"], preferred_element_type=jnp.float32
        )
    )
    normed_grad = lax.psum_scatter(
        normed_terms.astype(jnp.bfloat16), "tensor", scatter_dimension=1, tiled=True
    ).astype(jnp.float32)
    first_pull = jax.vjp(layer_norm, saved["rows"], saved["gain_one"], saved["bias_one"])[1]
    tokens_part, gain_one_grad, bias_one_grad = first_pull(normed_grad)
    tokens_grad = middle_grad + tokens_part
    summed = lax.psum(
        (
            gain_one_grad,
            bias_one_grad,
            out_shift_grad,
            gain_two_grad,
            bias_two_grad,
            down_shift_grad,
        ),
        "tensor",
    )
    owned = (
        lax.psum_scatter(
            query_weight_grad.astype(jnp.bfloat16), "dp", scatter_dimension=0, tiled=True
        ).astype(jnp.float32),
        lax.psum_scatter(
            key_weight_grad.astype(jnp.bfloat16), "dp", scatter_dimension=0, tiled=True
        ).astype(jnp.float32),
        lax.psum_scatter(
            value_weight_grad.astype(jnp.bfloat16), "dp", scatter_dimension=0, tiled=True
        ).astype(jnp.float32),
        lax.psum_scatter(
            out_grad.astype(jnp.bfloat16), "dp", scatter_dimension=0, tiled=True
        ).astype(jnp.float32),
        lax.psum_scatter(
            summed[0].astype(jnp.bfloat16), "dp", scatter_dimension=0, tiled=True
        ).astype(jnp.float32),
        lax.psum_scatter(
            summed[1].astype(jnp.bfloat16), "dp", scatter_dimension=0, tiled=True
        ).astype(jnp.float32),
        lax.psum_scatter(
            summed[2].astype(jnp.bfloat16), "dp", scatter_dimension=0, tiled=True
        ).astype(jnp.float32),
        lax.psum_scatter(
            summed[3].astype(jnp.bfloat16), "dp", scatter_dimension=0, tiled=True
        ).astype(jnp.float32),
        lax.psum_scatter(
            summed[4].astype(jnp.bfloat16), "dp", scatter_dimension=0, tiled=True
        ).astype(jnp.float32),
        lax.psum_scatter(
            summed[5].astype(jnp.bfloat16), "dp", scatter_dimension=0, tiled=True
        ).astype(jnp.float32),
    )
    shared = lax.psum((query_shift_grad, value_shift_grad, up_shift_grad), "dp")
    return (
        first["output"].astype(jnp.bfloat16),
        tokens_grad,
        owned[4],
        owned[5],
        owned[0],
        shared[0],
        owned[1],
        owned[2],
        shared[1],
        owned[3],
        owned[6],
        owned[7],
        owned[8],
        up_grad_shard,
        shared[2],
        down_grad_shard,
        owned[9],
    )


def solution(mesh):
    placed = (
        P("dp", "tensor", None),
        P("dp"),
        P("dp", "tensor", None),
        P("dp"),
        P("dp"),
        P("dp", "tensor"),
        P("tensor"),
        P("dp", "tensor"),
        P("dp", "tensor"),
        P("tensor"),
        P("dp", "tensor"),
        P("dp"),
        P("dp"),
        P("dp"),
        P("dp", "tensor"),
        P("tensor"),
        P("dp", "tensor"),
        P("dp"),
    )
    return jax.shard_map(
        local,
        mesh=mesh,
        in_specs=placed,
        out_specs=(
            P("dp", "tensor", None),
            P("dp", "tensor", None),
            P("dp"),
            P("dp"),
            P("dp", "tensor"),
            P("tensor"),
            P("dp", "tensor"),
            P("dp", "tensor"),
            P("tensor"),
            P("dp", "tensor"),
            P("dp"),
            P("dp"),
            P("dp"),
            P("dp", "tensor"),
            P("tensor"),
            P("dp", "tensor"),
            P("dp"),
        ),
        check_vma=False,
    )
```

profile of v0, /device:TPU:0, one launch (start us, length us, event | category | flops | bytes accessed | tf_op | source)
XLA Modules:
  0.0 1138.2 jit_solution(9833556908998333741)
XLA Ops:
  15.2 25.5 %all-reduce.21 = (bf16[1280]{0:T(1024)(128)(2,1)S(1)}, bf16[1280]{0:T(1024)(128)(2,1)S(1)}, bf16[1280]{0:T(1024)(128)(2,1)S(1)}, bf16[1280]{0:T(1024)(128)(2,1)S...) all-reduce(bf16[1280]{0:T(1024)(128)(2,1)S(1)} %dynamic-update-slic, ...), channel_id=1, replica_groups=mesh['dp'=8,'tensor'=4] {'dp'}, use_global_device_ids=true, to_apply=%add.1 | all-reduce | flops 7680 | bytes 30720
  109.7 25.4 %while.64 = (s32[]{:T(128)}, bf16[2,512,4,80]{1,3,2,0:T(8,128)(2,1)S(1)}, s32[]{:T(128)}, bf16[2,512,4,80]{1,3,2,0:T(8,128)(2,1)S(1)}, bf16[1024,4,80]{0,2,1:T(8...) while((s32[]{:T(128)}, bf16[2,512,4,80]{1,3,2,0:T(8,128)(2,1)S(1)}, s32[]{:T(128)}, ...), condition=%wide.region_5.6_spmd, body=%wide.region_2.5_spmd.sunk | while | flops 683837440 | bytes 21383284 | solution.py:41
  140.3 49.8 %reduce-scatter.14.cloned.1.call-done = bf16[1,256,1280]{2,1,0:T(8,128)(2,1)} async-done(((bf16[1,1024,1280]{2,1,0:T(8,128)(2,1)}), bf16[1,256,1280]{2,1,0:T(8,128)(2,1)}) %reduce-scatter.14.cloned.1.call-update) | async-done | bytes 655376 | tf_op jit(solution)/shard_map/reduce_scatter | solution.py:153
  207.3 56.7 %all-gather.13.cloned.1.call-done = bf16[1,1024,1280]{2,1,0:T(8,128)(2,1)} async-done(((bf16[1,256,1280]{2,1,0:T(8,128)(2,1)}), bf16[1,1024,1280]{2,1,0:T(8,128)(2,1)}) %all-gather.13.cloned.1.call-update) | async-done | bytes 2621456 | tf_op jit(solution)/shard_map/all_gather | solution.py:167
  264.0 21.3 %fusion.96 = bf16[1,1024,1280]{2,1,0:T(8,128)(2,1)} fusion(bf16[1280,1280]{1,0:T(8,128)(2,1)} %all-gather.17.cloned.1.call-done, bf16[1280,1280]{1,0:T(8,128)(2,1)} %all-gather.15.cloned.1.call-done, bf16[1,1024,1280]{2,1,0:T(8,128)(2,1)} %all-gather.13.cloned.1.call-done, f32[1280]{0:T(1024)S(1)} %convert_element_type.308), kind=kOutput, calls=%fused_computation.127 | convolution fusion | flops 6798704640 | bytes 11801600 | tf_op jit(solution)/shard_map/csf,df->csd/dot_general | solution.py:172
  285.5 50.9 %reduce-scatter.16.cloned.1.call-done = bf16[1,256,1280]{2,1,0:T(8,128)(2,1)} async-done(((bf16[1,1024,1280]{2,1,0:T(8,128)(2,1)}), bf16[1,256,1280]{2,1,0:T(8,128)(2,1)}) %reduce-scatter.16.cloned.1.call-update) | async-done | bytes 655376 | tf_op jit(solution)/shard_map/reduce_scatter | solution.py:173
  340.5 23.8 %all-reduce.20 = (bf16[1280]{0:T(1024)(128)(2,1)S(1)}, bf16[1280]{0:T(1024)(128)(2,1)S(1)}, bf16[1280]{0:T(1024)(128)(2,1)S(1)}, bf16[1280]{0:T(1024)(128)(2,1)S(1)}, bf16[1280]{0:T(1024)(128)(2,1)S(1)}) all-reduce(bf16[1280]{0:T(1024)(128)(2,1)S(1)} %dynamic-update-slice.10, ...), channel_id=1, replica_groups=mesh['dp'=8,'tensor'=4] {'dp'}, use_global_device_ids=true, to_apply=%add.10 | all-reduce | flops 6400 | bytes 25600
  430.5 13.7 %while.65 = (s32[]{:T(128)}, bf16[2,512,4,80]{1,3,2,0:T(8,128)(2,1)S(1)}, f32[2,4,512]{2,1,0:T(4,128)S(1)}, s32[]{:T(128)}, bf16[2,512,4,80]{1,3,2,0:T(8,128)(2,...) while((s32[]{:T(128)}, ...), condition=%wide.region_15.16_spmd, body=%wide.region_12.15_spmd.sunk | while | flops 696417280 | bytes 27201636 | solution.py:41
  451.0 50.2 %reduce-scatter.18.cloned.1.call-done = bf16[1,256,1280]{2,1,0:T(8,128)(2,1)} async-done(((bf16[1,1024,1280]{2,1,0:T(8,128)(2,1)}), bf16[1,256,1280]{2,1,0:T(8,128)(2,1)}) %reduce-scatter.18.cloned.1.call-update) | async-done | bytes 655376 | tf_op jit(solution)/shard_map/reduce_scatter | solution.py:153
  507.6 27.8 %all-gather.23.cloned.1.call-done = bf16[1280,1280]{1,0:T(8,128)(2,1)} async-done(((bf16[160,1280]{1,0:T(8,128)(2,1)}), bf16[1280,1280]{1,0:T(8,128)(2,1)}) %all-gather.23.cloned.1.call-update) | async-done | bytes 3276816 | tf_op jit(solution)/shard_map/all_gather | solution.py:158
  535.4 56.8 %all-gather.21.cloned.1.call-done = bf16[1,1024,1280]{2,1,0:T(8,128)(2,1)} async-done(((bf16[1,256,1280]{2,1,0:T(8,128)(2,1)}), bf16[1,1024,1280]{2,1,0:T(8,128)(2,1)}) %all-gather.21.cloned.1.call-update) | async-done | bytes 2621456 | tf_op jit(solution)/shard_map/all_gather | solution.py:167
  592.3 17.6 %fusion.75 = (f32[1024,1280]{1,0:T(8,128)}, f32[1024,1280]{1,0:T(8,128)}) fusion(f32[1280]{0:T(1024)S(1)} %convert_element_type.332, bf16[1280,1280]{1,0:T(8,128)(2,1)} %all-gather.23.cloned.1.call-done, bf16[1,1024,1280]{2,1,0:T(8,128)(2,1)} %all-gather.21.cloned.1.call-done), kind=kOutput, calls=%fused_computation.81 | convolution fusion | flops 3438018560 | bytes 16389120 | tf_op jit(solution)/shard_map/csd,df->csf/dot_general | solution.py:168
  609.9 37.3 %all-gather.27.cloned.1.call-done = bf16[1,1024,1280]{2,1,0:T(8,128)(2,1)} async-done(((bf16[1,256,1280]{2,1,0:T(8,128)(2,1)}), bf16[1,1024,1280]{2,1,0:T(8,128)(2,1)}) %all-gather.27.cloned.1.call-update) | async-done | bytes 2621456 | tf_op jit(solution)/shard_map/all_gather | solution.py:249
  647.1 33.2 %all-gather.25.cloned.1.call-done = bf16[1280,1280]{1,0:T(8,128)(2,1)} async-done(((bf16[160,1280]{1,0:T(8,128)(2,1)}), bf16[1280,1280]{1,0:T(8,128)(2,1)}) %all-gather.25.cloned.1.call-update) | async-done | bytes 3276816 | tf_op jit(solution)/shard_map/all_gather | solution.py:159
  698.2 52.2 %reduce-scatter.20.cloned.1.call-done = bf16[1,256,1280]{2,1,0:T(8,128)(2,1)} async-done(((bf16[1,1024,1280]{2,1,0:T(8,128)(2,1)}), bf16[1,256,1280]{2,1,0:T(8,128)(2,1)}) %reduce-scatter.20.cloned.1.call-update) | async-done | bytes 655376 | tf_op jit(solution)/shard_map/reduce_scatter | solution.py:273
  783.2 30.0 %all-gather.29.cloned.1.call-done = bf16[1,1024,1280]{2,1,0:T(8,128)(2,1)} async-done(((bf16[1,256,1280]{2,1,0:T(8,128)(2,1)}), bf16[1,1024,1280]{2,1,0:T(8,128)(2,1)}) %all-gather.29.cloned.1.call-update) | async-done | bytes 2621456 | tf_op jit(solution)/shard_map/all_gather | solution.py:280
  823.2 41.3 %while.66 = (s32[]{:T(128)}, f32[1024,4,80]{0,2,1:T(8,128)S(1)}, f32[1024,4,80]{0,2,1:T(8,128)}, bf16[2,512,4,80]{1,3,2,0:T(8,128)(2,1)}, bf16[2,512,4,80]{1,3,2...) while((s32[]{:T(128)}, f32[1024,4,80]{0,2,1:T(8,128)S(1)}, ...), condition=%wide.region_24.25_spmd.clone, body=%wide.region_22.24_spmd.clone.sunk | while | flops 1711143936 | bytes 144175888 | solution.py:79
  899.7 24.7 %all-reduce.17 = (f32[320]{0:T(512)}, f32[320]{0:T(512)}, f32[1280]{0:T(1024)}) all-reduce(f32[320]{0:T(512)S(1)} %reduce_sum.247, f32[320]{0:T(512)S(1)} %reduce_sum.249, f32[1280]{0:T(1024)S(1)} %copy-done.43), channel_id=1, replica_groups=mesh['dp'=8,'tensor'=4] {'dp'}, use_global_device_ids=true, to_apply=%region_36.37 | all-reduce | flops 1920 | bytes 15360 | tf_op jit(solution)/shard_map/psum | solution.py:378
  926.0 23.7 %reduce-scatter.26.cloned.1.call-done = bf16[160,320]{1,0:T(8,128)(2,1)} async-done(((bf16[1280,320]{1,0:T(8,128)(2,1)}), bf16[160,320]{1,0:T(8,128)(2,1)}) %reduce-scatter.26.cloned.1.call-update) | async-done | bytes 102416 | tf_op jit(solution)/shard_map/reduce_scatter | solution.py:350
  951.2 37.2 %reduce-scatter.30.cloned.1.call-done = bf16[160,320]{1,0:T(8,128)(2,1)} async-done(((bf16[1280,320]{1,0:T(8,128)(2,1)}), bf16[160,320]{1,0:T(8,128)(2,1)}) %reduce-scatter.30.cloned.1.call-update) | async-done | bytes 102416 | tf_op jit(solution)/shard_map/reduce_scatter | solution.py:356
  990.1 37.6 %reduce-scatter.24.cloned.1.call-done = bf16[160,320]{1,0:T(8,128)(2,1)} async-done(((bf16[1280,320]{1,0:T(8,128)(2,1)}), bf16[160,320]{1,0:T(8,128)(2,1)}) %reduce-scatter.24.cloned.1.call-update) | async-done | bytes 102416 | tf_op jit(solution)/shard_map/reduce_scatter | solution.py:347
  1029.3 52.9 %reduce-scatter.22.cloned.1.call-done = bf16[1,256,1280]{2,1,0:T(8,128)(2,1)} async-done(((bf16[1,1024,1280]{2,1,0:T(8,128)(2,1)}), bf16[1,256,1280]{2,1,0:T(8,128)(2,1)}) %reduce-scatter.22.cloned.1.call-update) | async-done | bytes 655376 | tf_op jit(solution)/shard_map/reduce_scatter | solution.py:329
  1085.6 17.8 %all-reduce.18 = (bf16[1280]{0:T(1024)(128)(2,1)S(1)}, bf16[1280]{0:T(1024)(128)(2,1)S(1)}, bf16[1280]{0:T(1024)(128)(2,1)S(1)}, bf16[1280]{0:T(1024)(128)(2,1)S...) all-reduce(f32[1280]{0:T(1024)S(1)} %get-tuple-element.403, ...), channel_id=1, replica_groups=mesh['dp'=8,'tensor'=4] {'tensor'}, use_global_device_ids=true, to_apply=%region_29.30 | all-reduce | flops 7680 | bytes 46080 | tf_op jit(solution)/shard_map/psum | solution.py:335
  1103.3 22.4 %all-reduce.19 = (bf16[1280]{0:T(1024)(128)(2,1)S(1)}, bf16[1280]{0:T(1024)(128)(2,1)S(1)}, bf16[1280]{0:T(1024)(128)(2,1)S(1)}, bf16[1280]{0:T(1024)(128)(2,1)S...) all-reduce(bf16[1280]{0:T(1024)(128)(2,1)S(1)} %get-tuple-element.4, ...), channel_id=7, replica_groups=mesh['dp'=8,'tensor'=4] {'dp'}, use_global_device_ids=true, to_apply=%region_30.31.clone | all-reduce | flops 7680 | bytes 30720
  (341 shorter events, 370.1 us)
Async XLA Ops:
  8.1 92.0 %all-gather.11.cloned.1.call-start = ((), (), s32[]{:S(2)}) async-start(), calls=%async_computation.11 | async-start | bytes 3276800 | tf_op jit(solution)/shard_map/all_gather | solution.py:120
  45.7 144.3 %reduce-scatter.14.cloned.1.call-start = ((), (), s32[]{:S(2)}) async-start(), calls=%async_computation.12 | async-start | bytes 3276800 | tf_op jit(solution)/shard_map/reduce_scatter | solution.py:153
  139.0 56.7 %all-gather.15.cloned.1.call-start = ((), (), s32[]{:S(2)}) async-start(), calls=%async_computation.14 | async-start | bytes 3686400 | tf_op jit(solution)/shard_map/all_gather | solution.py:158
  139.6 67.7 %all-gather.17.cloned.1.call-start = ((), (), s32[]{:S(2)}) async-start(), calls=%async_computation.15 | async-start | bytes 3686400 | tf_op jit(solution)/shard_map/all_gather | solution.py:159
  140.2 123.8 %all-gather.13.cloned.1.call-start = ((), (), s32[]{:S(2)}) async-start(), calls=%async_computation.13 | async-start | bytes 3276800 | tf_op jit(solution)/shard_map/all_gather | solution.py:167
  195.3 141.2 %reduce-scatter.16.cloned.1.call-start = ((), (), s32[]{:S(2)}) async-start(), calls=%async_computation.16 | async-start | bytes 3276800 | tf_op jit(solution)/shard_map/reduce_scatter | solution.py:173
  285.4 133.1 %all-gather.19.cloned.1.call-start = ((), (), s32[]{:S(2)}) async-start(), calls=%async_computation.17 | async-start | bytes 3276800 | tf_op jit(solution)/shard_map/all_gather | solution.py:120
  365.5 135.7 %reduce-scatter.18.cloned.1.call-start = ((), (), s32[]{:S(2)}) async-start(), calls=%async_computation.18 | async-start | bytes 3276800 | tf_op jit(solution)/shard_map/reduce_scatter | solution.py:153
  450.2 85.2 %all-gather.23.cloned.1.call-start = ((), (), s32[]{:S(2)}) async-start(), calls=%async_computation.20 | async-start | bytes 3686400 | tf_op jit(solution)/shard_map/all_gather | solution.py:158
  451.0 141.3 %all-gather.21.cloned.1.call-start = ((), (), s32[]{:S(2)}) async-start(), calls=%async_computation.19 | async-start | bytes 3276800 | tf_op jit(solution)/shard_map/all_gather | solution.py:167
  506.4 140.7 %all-gather.27.cloned.1.call-start = ((), (), s32[]{:S(2)}) async-start(), calls=%async_computation.22 | async-start | bytes 3276800 | tf_op jit(solution)/shard_map/all_gather | solution.py:249
  507.0 173.4 %all-gather.25.cloned.1.call-start = ((), (), s32[]{:S(2)}) async-start(), calls=%async_computation.21 | async-start | bytes 3686400 | tf_op jit(solution)/shard_map/all_gather | solution.py:159
  507.6 242.8 %reduce-scatter.20.cloned.1.call-start = ((), (), s32[]{:S(2)}) async-start(), calls=%async_computation.23 | async-start | bytes 3276800 | tf_op jit(solution)/shard_map/reduce_scatter | solution.py:273
  698.2 115.0 %all-gather.29.cloned.1.call-start = ((), (), s32[]{:S(2)}) async-start(), calls=%async_computation.24 | async-start | bytes 3276800 | tf_op jit(solution)/shard_map/all_gather | solution.py:280
  758.6 135.2 %reduce-scatter.34.cloned.1.call-start = ((), (), s32[]{:S(2)}) async-start(), calls=%async_computation.31 | async-start | bytes 3686400
  774.9 121.3 %reduce-scatter.32.cloned.1.call-start = ((), (), s32[]{:S(2)}) async-start(), calls=%async_computation.30 | async-start | bytes 3686400 | tf_op jit(solution)/shard_map/reduce_scatter | solution.py:263
  782.9 141.4 %reduce-scatter.28.cloned.1.call-start = ((), (), s32[]{:S(2)}) async-start(), calls=%async_computation.28 | async-start | bytes 1105920 | tf_op jit(solution)/shard_map/reduce_scatter | solution.py:353
  871.1 78.6 %reduce-scatter.26.cloned.1.call-start = ((), (), s32[]{:S(2)}) async-start(), calls=%async_computation.27 | async-start | bytes 1105920 | tf_op jit(solution)/shard_map/reduce_scatter | solution.py:350
  875.8 112.6 %reduce-scatter.30.cloned.1.call-start = ((), (), s32[]{:S(2)}) async-start(), calls=%async_computation.29 | async-start | bytes 1105920 | tf_op jit(solution)/shard_map/reduce_scatter | solution.py:356
  880.2 147.5 %reduce-scatter.24.cloned.1.call-start = ((), (), s32[]{:S(2)}) async-start(), calls=%async_computation.26 | async-start | bytes 1105920 | tf_op jit(solution)/shard_map/reduce_scatter | solution.py:347
  886.5 195.6 %reduce-scatter.22.cloned.1.call-start = ((), (), s32[]{:S(2)}) async-start(), calls=%async_computation.25 | async-start | bytes 3276800 | tf_op jit(solution)/shard_map/reduce_scatter | solution.py:329
  896.1 189.4 %copy-start.36 = (f32[1280]{0:T(1024)S(1)}, f32[1280]{0:T(1024)}, u32[]{:S(2)}) copy-start(f32[1280]{0:T(1024)} %get-tuple-element.483) | copy-start | bytes 15364
  896.1 189.4 %copy-start.37 = (f32[1280]{0:T(1024)S(1)}, f32[1280]{0:T(1024)}, u32[]{:S(2)}) copy-start(f32[1280]{0:T(1024)} %get-tuple-element.491) | copy-start | bytes 15364
  896.1 231.6 %copy-start.8 = (f32[1,256,1280]{2,1,0:T(8,128)S(1)}, f32[1,256,1280]{2,1,0:T(8,128)}, u32[]{:S(2)}) copy-start(f32[1,256,1280]{2,1,0:T(8,128)} %copy-done.7) | copy-start | bytes 3932164
  (60 other events, 2784.7 us)
Sparse Core Ops, SparseCore 0:
  45.8 54.1 all-gather.10
  139.1 50.8 reduce-scatter.13
  285.5 50.8 reduce-scatter.15
  365.6 52.9 all-gather.18
  698.3 52.0 reduce-scatter.19
  758.7 54.4 all-gather.28
Sparse Core Ops, SparseCore 1:
  141.4 31.4 all-gather.14
  174.6 32.7 all-gather.16
  209.4 54.6 all-gather.12
  450.3 50.9 reduce-scatter.17
  503.1 32.2 all-gather.22
  537.6 54.6 all-gather.20
  593.7 53.4 all-gather.26
  648.9 31.4 all-gather.24
  775.0 46.4 reduce-scatter.33
  824.8 46.7 reduce-scatter.31
  874.7 35.6 reduce-scatter.27
  913.9 35.6 reduce-scatter.25
  952.7 35.7 reduce-scatter.29
  992.0 35.6 reduce-scatter.23
  1030.0 52.1 reduce-scatter.21
where the time goes:
time: 1140 us
  waiting for transfers between devices  629 us (55%)
  blocking collectives  203 us (18%)
  matrix products  190 us (17%)
  other arithmetic  61 us (5%)
  local copies, waits for them, and re-layouts  34.6 us (3%)
  between operations  18.4 us (2%)
    all_gather x2, waiting for transfers between devices, forward_pass(): normed_two_all = lax.all_gather(normed_two, 'tensor', axis=1, tiled=True)  114 us
    reduce_scatter x2, waiting for transfers between devices, forward_pass(): lax.psum_scatter(attn_terms.astype(jnp.bfloat16), 'tensor', scatter_dimen...  99.9 us
    unnamed x3, blocking collectives  71.7 us
    reduce_scatter x1, waiting for transfers between devices, local(): lax.psum_scatter(normed_terms.astype(jnp.bfloat16), 'tensor', scatter_dim...  52.9 us
    reduce_scatter x1, waiting for transfers between devices, local(): lax.psum_scatter(normed_two_terms.astype(jnp.bfloat16), 'tensor', scatter...  52.2 us
    reduce_scatter x1, waiting for transfers between devices, forward_pass(): lax.psum_scatter(mlp_terms.astype(jnp.bfloat16), 'tensor', scatter_dimens...  50.9 us
    all_gather x2, waiting for transfers between devices, forward_pass(): lax.all_gather(down_weight, 'dp', axis=0, tiled=True)  44.8 us
    reduce_scatter x1, waiting for transfers between devices, local(): lax.psum_scatter(query_weight_grad.astype(jnp.bfloat16), 'dp', scatter_di...  37.6 us
  transfers between devices with their start and end apart: 21, of which 17 were waited for; matrix products, arithmetic and copies ran while one was open for 12% of the time, Pallas kernels for 0%

commit v1 on v0

--- a/solution.py
+++ b/solution.py
@@ -246,7 +246,14 @@
     blocks = saved["blocks"]
     grad_out = cotangent.astype(jnp.float32)
     down_shift_grad = jnp.sum(grad_out, axis=(0, 1))
-    grad_out_all = lax.all_gather(cotangent, "tensor", axis=1, tiled=True)
+    ring = [cotangent]
+    for hop in range(3):
+        ring.append(lax.ppermute(ring[-1], "tensor", [(dev, (dev + 1) % 4) for dev in range(4)]))
+    grad_out_all = jnp.roll(
+        jnp.concatenate(ring[::-1], axis=1),
+        (lax.axis_index("tensor") + 1) * ring[0].shape[1],
+        axis=1,
+    )
     down_grad = jnp.einsum(
         "csd,csf->df", grad_out_all, saved["hidden"], preferred_element_type=jnp.float32
     )

time: 1140 us -> 1090 us (0.956)
  waiting for transfers between devices: 629 us -> 571 us
    ppermute x0 -> x3, waiting for transfers between devices: none -> 62.3 us  [local(): lax.ppermute(ring[-1], 'tensor', [(dev, (dev + 1) % 4) for dev in range(4)])]
    all_gather x1 -> x0, waiting for transfers between devices: 37.3 us -> none  [local(): grad_out_all = lax.all_gather(cotangent, 'tensor', axis=1, tiled=True)]
    all_gather x2, waiting for transfers between devices: 114 us -> 76.4 us  [forward_pass(): normed_two_all = lax.all_gather(normed_two, 'tensor', axis=1, tiled=True)]
    all_gather x2, waiting for transfers between devices: 27.8 us -> 0.03 us  [forward_pass(): lax.all_gather(up_weight, 'dp', axis=0, tiled=True)]
    all_gather x2, waiting for transfers between devices: 44.8 us -> 26.6 us  [forward_pass(): lax.all_gather(down_weight, 'dp', axis=0, tiled=True)]
    unnamed x136 -> x134, local copies, waits for them, and re-layouts: 22.4 us -> 25 us
  transfers between devices with their start and end apart: 21 -> 23, of which waited for: 17 -> 18; matrix products, arithmetic and copies ran while one was open for 12% -> 14% of each run, Pallas kernels for 0% -> 0%
where the time goes in v1:
time: 1090 us
  waiting for transfers between devices  571 us (52%)
  blocking collectives  203 us (19%)
  matrix products  188 us (17%)
  other arithmetic  64.1 us (6%)
  local copies, waits for them, and re-layouts  38.1 us (3%)
  between operations  18.4 us (2%)
    reduce_scatter x2, waiting for transfers between devices, forward_pass(): lax.psum_scatter(attn_terms.astype(jnp.bfloat16), 'tensor', scatter_dimen...  99.9 us
    all_gather x2, waiting for transfers between devices, forward_pass(): normed_two_all = lax.all_gather(normed_two, 'tensor', axis=1, tiled=True)  76.4 us
    unnamed x3, blocking collectives  71.7 us
    ppermute x3, waiting for transfers between devices, local(): lax.ppermute(ring[-1], 'tensor', [(dev, (dev + 1) % 4) for dev in range(4)])  62.3 us
    reduce_scatter x1, waiting for transfers between devices, local(): lax.psum_scatter(normed_terms.astype(jnp.bfloat16), 'tensor', scatter_dim...  52.9 us
    reduce_scatter x1, waiting for transfers between devices, local(): lax.psum_scatter(normed_two_terms.astype(jnp.bfloat16), 'tensor', scatter...  52.2 us
    reduce_scatter x1, waiting for transfers between devices, forward_pass(): lax.psum_scatter(mlp_terms.astype(jnp.bfloat16), 'tensor', scatter_dimens...  50.9 us
    reduce_scatter x1, waiting for transfers between devices, local(): lax.psum_scatter(query_weight_grad.astype(jnp.bfloat16), 'dp', scatter_di...  37.5 us
  transfers between devices with their start and end apart: 23, of which 18 were waited for; matrix products, arithmetic and copies ran while one was open for 14% of the time, Pallas kernels for 0%

profile of v1, /device:TPU:0, one launch (start us, length us, event | category | flops | bytes accessed | tf_op | source)
XLA Modules:
  0.0 1085.7 jit_solution(14582369504636904582)
XLA Ops:
  15.2 25.5 %all-reduce.21 = (bf16[1280]{0:T(1024)(128)(2,1)S(1)}, bf16[1280]{0:T(1024)(128)(2,1)S(1)}, bf16[1280]{0:T(1024)(128)(2,1)S(1)}, bf16[1280]{0:T(1024)(128)(2,1)S...) all-reduce(bf16[1280]{0:T(1024)(128)(2,1)S(1)} %dynamic-update-slic, ...), channel_id=1, replica_groups=mesh['dp'=8,'tensor'=4] {'dp'}, use_global_device_ids=true, to_apply=%add.1 | all-reduce | flops 7680 | bytes 30720
  109.6 25.3 %while.64 = (s32[]{:T(128)}, bf16[2,512,4,80]{1,3,2,0:T(8,128)(2,1)S(1)}, s32[]{:T(128)}, bf16[2,512,4,80]{1,3,2,0:T(8,128)(2,1)S(1)}, bf16[1024,4,80]{0,2,1:T(8...) while((s32[]{:T(128)}, bf16[2,512,4,80]{1,3,2,0:T(8,128)(2,1)S(1)}, s32[]{:T(128)}, ...), condition=%wide.region_5.6_spmd, body=%wide.region_2.5_spmd.sunk | while | flops 683837440 | bytes 21383284 | solution.py:41
  140.2 49.8 %reduce-scatter.12.cloned.1.call-done = bf16[1,256,1280]{2,1,0:T(8,128)(2,1)} async-done(((bf16[1,1024,1280]{2,1,0:T(8,128)(2,1)}), bf16[1,256,1280]{2,1,0:T(8,128)(2,1)}) %reduce-scatter.12.cloned.1.call-update) | async-done | bytes 655376 | tf_op jit(solution)/shard_map/reduce_scatter | solution.py:153
  207.2 56.7 %all-gather.12.cloned.1.call-done = bf16[1,1024,1280]{2,1,0:T(8,128)(2,1)} async-done(((bf16[1,256,1280]{2,1,0:T(8,128)(2,1)}), bf16[1,1024,1280]{2,1,0:T(8,128)(2,1)}) %all-gather.12.cloned.1.call-update) | async-done | bytes 2621456 | tf_op jit(solution)/shard_map/all_gather | solution.py:167
  263.9 21.3 %fusion.88 = bf16[1,1024,1280]{2,1,0:T(8,128)(2,1)} fusion(bf16[1280,1280]{1,0:T(8,128)(2,1)} %all-gather.16.cloned.1.call-done, bf16[1280,1280]{1,0:T(8,128)(2,1)} %all-gather.14.cloned.1.call-done, bf16[1,1024,1280]{2,1,0:T(8,128)(2,1)} %all-gather.12.cloned.1.call-done, f32[1280]{0:T(1024)S(1)} %convert_element_type.305), kind=kOutput, calls=%fused_computation.118 | convolution fusion | flops 6798704640 | bytes 11801600 | tf_op jit(solution)/shard_map/csf,df->csd/dot_general | solution.py:172
  285.4 50.9 %reduce-scatter.14.cloned.1.call-done = bf16[1,256,1280]{2,1,0:T(8,128)(2,1)} async-done(((bf16[1,1024,1280]{2,1,0:T(8,128)(2,1)}), bf16[1,256,1280]{2,1,0:T(8,128)(2,1)}) %reduce-scatter.14.cloned.1.call-update) | async-done | bytes 655376 | tf_op jit(solution)/shard_map/reduce_scatter | solution.py:173
  340.5 23.8 %all-reduce.20 = (bf16[1280]{0:T(1024)(128)(2,1)S(1)}, bf16[1280]{0:T(1024)(128)(2,1)S(1)}, bf16[1280]{0:T(1024)(128)(2,1)S(1)}, bf16[1280]{0:T(1024)(128)(2,1)S(1)}, bf16[1280]{0:T(1024)(128)(2,1)S(1)}) all-reduce(bf16[1280]{0:T(1024)(128)(2,1)S(1)} %dynamic-update-slice.10, ...), channel_id=1, replica_groups=mesh['dp'=8,'tensor'=4] {'dp'}, use_global_device_ids=true, to_apply=%add.10 | all-reduce | flops 6400 | bytes 25600
  451.0 50.1 %reduce-scatter.16.cloned.1.call-done = bf16[1,256,1280]{2,1,0:T(8,128)(2,1)} async-done(((bf16[1,1024,1280]{2,1,0:T(8,128)(2,1)}), bf16[1,256,1280]{2,1,0:T(8,128)(2,1)}) %reduce-scatter.16.cloned.1.call-update) | async-done | bytes 655376 | tf_op jit(solution)/shard_map/reduce_scatter | solution.py:153
  507.2 17.4 %collective-permute-done = bf16[1,256,1280]{2,1,0:T(8,128)(2,1)S(1)} collective-permute-done((bf16[1,256,1280]{2,1,0:T(8,128)(2,1)S(1)}, bf16[1,256,1280]{2,1,0:T(8,128)(2,1)S(1)}, u32[]{:S(2)}, u32[]{:S(2)}) %collective-permute-start) | collective-permute-done | bytes 655392 | tf_op jit(solution)/shard_map/ppermute | solution.py:251
  524.6 17.1 %collective-permute-done.1 = bf16[1,256,1280]{2,1,0:T(8,128)(2,1)} collective-permute-done((bf16[1,256,1280]{2,1,0:T(8,128)(2,1)S(1)}, bf16[1,256,1280]{2,1,0:T(8,128)(2,1)}, u32[]{:S(2)}, u32[]{:S(2)}) %collective-permute-start.1) | collective-permute-done | bytes 655392 | tf_op jit(solution)/shard_map/ppermute | solution.py:251
  541.8 27.8 %collective-permute-done.2 = bf16[1,256,1280]{2,1,0:T(8,128)(2,1)} collective-permute-done((bf16[1,256,1280]{2,1,0:T(8,128)(2,1)}, bf16[1,256,1280]{2,1,0:T(8,128)(2,1)}, u32[]{:S(2)}, u32[]{:S(2)}) %collective-permute-start.2) | collective-permute-done | bytes 655392 | tf_op jit(solution)/shard_map/ppermute | solution.py:251
  581.2 19.7 %all-gather.20.cloned.1.call-done = bf16[1,1024,1280]{2,1,0:T(8,128)(2,1)} async-done(((bf16[1,256,1280]{2,1,0:T(8,128)(2,1)}), bf16[1,1024,1280]{2,1,0:T(8,128)(2,1)}) %all-gather.20.cloned.1.call-update) | async-done | bytes 2621456 | tf_op jit(solution)/shard_map/all_gather | solution.py:167
  600.9 17.6 %fusion.74 = (f32[1024,1280]{1,0:T(8,128)}, f32[1024,1280]{1,0:T(8,128)}) fusion(f32[1280]{0:T(1024)S(1)} %convert_element_type.329, bf16[1280,1280]{1,0:T(8,128)(2,1)} %all-gather.22.cloned.1.call-done, bf16[1,1024,1280]{2,1,0:T(8,128)(2,1)} %all-gather.20.cloned.1.call-done), kind=kOutput, calls=%fused_computation.80 | convolution fusion | flops 3438018560 | bytes 16389120 | tf_op jit(solution)/shard_map/csd,df->csf/dot_general | solution.py:168
  618.5 15.1 %all-gather.24.cloned.1.call-done = bf16[1280,1280]{1,0:T(8,128)(2,1)} async-done(((bf16[160,1280]{1,0:T(8,128)(2,1)}), bf16[1280,1280]{1,0:T(8,128)(2,1)}) %all-gather.24.cloned.1.call-update) | async-done | bytes 3276816 | tf_op jit(solution)/shard_map/all_gather | solution.py:159
  651.4 52.2 %reduce-scatter.18.cloned.1.call-done = bf16[1,256,1280]{2,1,0:T(8,128)(2,1)} async-done(((bf16[1,1024,1280]{2,1,0:T(8,128)(2,1)}), bf16[1,256,1280]{2,1,0:T(8,128)(2,1)}) %reduce-scatter.18.cloned.1.call-update) | async-done | bytes 655376 | tf_op jit(solution)/shard_map/reduce_scatter | solution.py:280
  730.8 35.7 %all-gather.26.cloned.1.call-done = bf16[1,1024,1280]{2,1,0:T(8,128)(2,1)} async-done(((bf16[1,256,1280]{2,1,0:T(8,128)(2,1)}), bf16[1,1024,1280]{2,1,0:T(8,128)(2,1)}) %all-gather.26.cloned.1.call-update) | async-done | bytes 2621456 | tf_op jit(solution)/shard_map/all_gather | solution.py:287
  776.2 40.1 %while.66 = (s32[]{:T(128)}, f32[1024,4,80]{0,2,1:T(8,128)S(1)}, f32[1024,4,80]{0,2,1:T(8,128)}, bf16[2,512,4,80]{1,3,2,0:T(8,128)(2,1)}, bf16[2,512,4,80]{1,3,2...) while((s32[]{:T(128)}, f32[1024,4,80]{0,2,1:T(8,128)S(1)}, ...), condition=%wide.region_24.25_spmd.clone, body=%wide.region_22.24_spmd.clone.sunk | while | flops 1711143936 | bytes 144175888 | solution.py:79
  851.1 24.1 %all-reduce.17 = (f32[320]{0:T(512)}, f32[320]{0:T(512)}, f32[1280]{0:T(1024)}) all-reduce(f32[320]{0:T(512)S(1)} %reduce_sum.247, f32[320]{0:T(512)S(1)} %reduce_sum.249, f32[1280]{0:T(1024)S(1)} %copy-done.42), channel_id=1, replica_groups=mesh['dp'=8,'tensor'=4] {'dp'}, use_global_device_ids=true, to_apply=%region_36.37 | all-reduce | flops 1920 | bytes 15360 | tf_op jit(solution)/shard_map/psum | solution.py:385
  876.8 20.3 %reduce-scatter.24.cloned.1.call-done = bf16[160,320]{1,0:T(8,128)(2,1)} async-done(((bf16[1280,320]{1,0:T(8,128)(2,1)}), bf16[160,320]{1,0:T(8,128)(2,1)}) %reduce-scatter.24.cloned.1.call-update) | async-done | bytes 102416 | tf_op jit(solution)/shard_map/reduce_scatter | solution.py:357
  898.7 37.3 %reduce-scatter.28.cloned.1.call-done = bf16[160,320]{1,0:T(8,128)(2,1)} async-done(((bf16[1280,320]{1,0:T(8,128)(2,1)}), bf16[160,320]{1,0:T(8,128)(2,1)}) %reduce-scatter.28.cloned.1.call-update) | async-done | bytes 102416 | tf_op jit(solution)/shard_map/reduce_scatter | solution.py:363
  937.7 37.5 %reduce-scatter.22.cloned.1.call-done = bf16[160,320]{1,0:T(8,128)(2,1)} async-done(((bf16[1280,320]{1,0:T(8,128)(2,1)}), bf16[160,320]{1,0:T(8,128)(2,1)}) %reduce-scatter.22.cloned.1.call-update) | async-done | bytes 102416 | tf_op jit(solution)/shard_map/reduce_scatter | solution.py:354
  976.8 52.9 %reduce-scatter.20.cloned.1.call-done = bf16[1,256,1280]{2,1,0:T(8,128)(2,1)} async-done(((bf16[1,1024,1280]{2,1,0:T(8,128)(2,1)}), bf16[1,256,1280]{2,1,0:T(8,128)(2,1)}) %reduce-scatter.20.cloned.1.call-update) | async-done | bytes 655376 | tf_op jit(solution)/shard_map/reduce_scatter | solution.py:336
  1033.1 17.7 %all-reduce.18 = (bf16[1280]{0:T(1024)(128)(2,1)S(1)}, bf16[1280]{0:T(1024)(128)(2,1)S(1)}, bf16[1280]{0:T(1024)(128)(2,1)S(1)}, bf16[1280]{0:T(1024)(128)(2,1)S...) all-reduce(f32[1280]{0:T(1024)S(1)} %get-tuple-element.352, ...), channel_id=1, replica_groups=mesh['dp'=8,'tensor'=4] {'tensor'}, use_global_device_ids=true, to_apply=%region_29.30 | all-reduce | flops 7680 | bytes 46080 | tf_op jit(solution)/shard_map/psum | solution.py:342
  1050.8 22.5 %all-reduce.19 = (bf16[1280]{0:T(1024)(128)(2,1)S(1)}, bf16[1280]{0:T(1024)(128)(2,1)S(1)}, bf16[1280]{0:T(1024)(128)(2,1)S(1)}, bf16[1280]{0:T(1024)(128)(2,1)S...) all-reduce(bf16[1280]{0:T(1024)(128)(2,1)S(1)} %get-tuple-element.4, ...), channel_id=7, replica_groups=mesh['dp'=8,'tensor'=4] {'dp'}, use_global_device_ids=true, to_apply=%region_30.31.clone | all-reduce | flops 7680 | bytes 30720
  (344 shorter events, 387.7 us)
Async XLA Ops:
  8.1 91.9 %all-gather.10.cloned.1.call-start = ((), (), s32[]{:S(2)}) async-start(), calls=%async_computation.11 | async-start | bytes 3276800 | tf_op jit(solution)/shard_map/all_gather | solution.py:120
  45.6 144.3 %reduce-scatter.12.cloned.1.call-start = ((), (), s32[]{:S(2)}) async-start(), calls=%async_computation.12 | async-start | bytes 3276800 | tf_op jit(solution)/shard_map/reduce_scatter | solution.py:153
  138.9 56.8 %all-gather.14.cloned.1.call-start = ((), (), s32[]{:S(2)}) async-start(), calls=%async_computation.14 | async-start | bytes 3686400 | tf_op jit(solution)/shard_map/all_gather | solution.py:158
  139.5 67.7 %all-gather.16.cloned.1.call-start = ((), (), s32[]{:S(2)}) async-start(), calls=%async_computation.15 | async-start | bytes 3686400 | tf_op jit(solution)/shard_map/all_gather | solution.py:159
  140.1 123.9 %all-gather.12.cloned.1.call-start = ((), (), s32[]{:S(2)}) async-start(), calls=%async_computation.13 | async-start | bytes 3276800 | tf_op jit(solution)/shard_map/all_gather | solution.py:167
  195.1 141.2 %reduce-scatter.14.cloned.1.call-start = ((), (), s32[]{:S(2)}) async-start(), calls=%async_computation.16 | async-start | bytes 3276800 | tf_op jit(solution)/shard_map/reduce_scatter | solution.py:173
  285.4 133.2 %all-gather.18.cloned.1.call-start = ((), (), s32[]{:S(2)}) async-start(), calls=%async_computation.17 | async-start | bytes 3276800 | tf_op jit(solution)/shard_map/all_gather | solution.py:120
  365.4 135.8 %reduce-scatter.16.cloned.1.call-start = ((), (), s32[]{:S(2)}) async-start(), calls=%async_computation.18 | async-start | bytes 3276800 | tf_op jit(solution)/shard_map/reduce_scatter | solution.py:153
  450.2 131.0 %all-gather.22.cloned.1.call-start = ((), (), s32[]{:S(2)}) async-start(), calls=%async_computation.20 | async-start | bytes 3686400 | tf_op jit(solution)/shard_map/all_gather | solution.py:158
  450.9 149.9 %all-gather.20.cloned.1.call-start = ((), (), s32[]{:S(2)}) async-start(), calls=%async_computation.19 | async-start | bytes 3276800 | tf_op jit(solution)/shard_map/all_gather | solution.py:167
  506.4 127.2 %all-gather.24.cloned.1.call-start = ((), (), s32[]{:S(2)}) async-start(), calls=%async_computation.21 | async-start | bytes 3686400 | tf_op jit(solution)/shard_map/all_gather | solution.py:159
  506.4 18.2 %collective-permute-start = (bf16[1,256,1280]{2,1,0:T(8,128)(2,1)S(1)}, bf16[1,256,1280]{2,1,0:T(8,128)(2,1)S(1)}, u32[]{:S(2)}, u32[]{:S(2)}) collective-permute-start(bf16[1,256,1280]{2,1,0:T(8,128)(2,1)S(1)} %copy-done.13), channel_id=1, source_target_pairs={{0,1},{1,2},{2,3},{3,0},{4,5},{5,6},{6,7},{7,4},{8,9},{9,10},{10,1... | collective-permute-start | bytes 1966088 | tf_op jit(solution)/shard_map/ppermute | solution.py:251
  524.6 17.1 %collective-permute-start.1 = (bf16[1,256,1280]{2,1,0:T(8,128)(2,1)S(1)}, bf16[1,256,1280]{2,1,0:T(8,128)(2,1)}, u32[]{:S(2)}, u32[]{:S(2)}) collective-permute-start(bf16[1,256,1280]{2,1,0:T(8,128)(2,1)S(1)} %collective-permute-done), channel_id=1, source_target_pairs={{0,1},{1,2},{2,3},{3,0},{4,5},{5,6},{6,7},{7,4},{8,9},{9,10},{10,1... | collective-permute-start | bytes 1966088 | tf_op jit(solution)/shard_map/ppermute | solution.py:251
  541.7 27.9 %collective-permute-start.2 = (bf16[1,256,1280]{2,1,0:T(8,128)(2,1)}, bf16[1,256,1280]{2,1,0:T(8,128)(2,1)}, u32[]{:S(2)}, u32[]{:S(2)}) collective-permute-start(bf16[1,256,1280]{2,1,0:T(8,128)(2,1)} %collective-permute-done.1), channel_id=1, source_target_pairs={{0,1},{1,2},{2,3},{3,0},{4,5},{5,6},{6,7},{7,4},{8,9},{9,10},{10,1... | collective-permute-start | bytes 1966088 | tf_op jit(solution)/shard_map/ppermute | solution.py:251
  541.8 161.9 %reduce-scatter.18.cloned.1.call-start = ((), (), s32[]{:S(2)}) async-start(), calls=%async_computation.22 | async-start | bytes 3276800 | tf_op jit(solution)/shard_map/reduce_scatter | solution.py:280
  651.3 115.1 %all-gather.26.cloned.1.call-start = ((), (), s32[]{:S(2)}) async-start(), calls=%async_computation.23 | async-start | bytes 3276800 | tf_op jit(solution)/shard_map/all_gather | solution.py:287
  711.8 134.0 %reduce-scatter.32.cloned.1.call-start = ((), (), s32[]{:S(2)}) async-start(), calls=%async_computation.30 | async-start | bytes 3686400 | tf_op jit(solution)/shard_map/reduce_scatter | solution.py:273
  722.5 125.2 %reduce-scatter.30.cloned.1.call-start = ((), (), s32[]{:S(2)}) async-start(), calls=%async_computation.29 | async-start | bytes 3686400 | tf_op jit(solution)/shard_map/reduce_scatter | solution.py:270
  730.5 144.6 %reduce-scatter.26.cloned.1.call-start = ((), (), s32[]{:S(2)}) async-start(), calls=%async_computation.27 | async-start | bytes 1105920 | tf_op jit(solution)/shard_map/reduce_scatter | solution.py:360
  822.9 74.2 %reduce-scatter.24.cloned.1.call-start = ((), (), s32[]{:S(2)}) async-start(), calls=%async_computation.26 | async-start | bytes 1105920 | tf_op jit(solution)/shard_map/reduce_scatter | solution.py:357
  827.7 108.4 %reduce-scatter.28.cloned.1.call-start = ((), (), s32[]{:S(2)}) async-start(), calls=%async_computation.28 | async-start | bytes 1105920 | tf_op jit(solution)/shard_map/reduce_scatter | solution.py:363
  832.1 143.1 %reduce-scatter.22.cloned.1.call-start = ((), (), s32[]{:S(2)}) async-start(), calls=%async_computation.25 | async-start | bytes 1105920 | tf_op jit(solution)/shard_map/reduce_scatter | solution.py:354
  838.5 191.2 %reduce-scatter.20.cloned.1.call-start = ((), (), s32[]{:S(2)}) async-start(), calls=%async_computation.24 | async-start | bytes 3276800 | tf_op jit(solution)/shard_map/reduce_scatter | solution.py:336
  844.9 230.3 %copy-start.8 = (f32[1,256,1280]{2,1,0:T(8,128)S(1)}, f32[1,256,1280]{2,1,0:T(8,128)}, u32[]{:S(2)}) copy-start(f32[1,256,1280]{2,1,0:T(8,128)} %copy-done.7) | copy-start | bytes 3932164
  (59 other events, 3175.0 us)
Sparse Core Ops, SparseCore 0:
  45.8 54.1 all-gather.9
  139.0 50.8 reduce-scatter.11
  285.5 50.8 reduce-scatter.13
  365.5 52.9 all-gather.17
  651.5 52.0 reduce-scatter.17
  711.9 54.4 all-gather.25
Sparse Core Ops, SparseCore 1:
  141.3 31.4 all-gather.13
  174.5 32.7 all-gather.15
  209.2 54.6 all-gather.11
  450.3 50.9 reduce-scatter.15
  503.1 32.2 all-gather.21
  537.5 63.3 all-gather.19
  602.6 30.9 all-gather.23
  722.6 46.4 reduce-scatter.31
  772.3 46.8 reduce-scatter.29
  823.0 34.9 reduce-scatter.25
  861.4 35.6 reduce-scatter.23
  900.4 35.6 reduce-scatter.27
  939.5 35.7 reduce-scatter.21
  977.5 52.1 reduce-scatter.19
